TPU v7x, 512 devices: a whole 4x8x8 slice. The times are simulated.
512 devices in a mesh: tm: 64 (over z, y), chan: 8 (over x, core).
Axes of the slice: x: 4, y: 8, z: 8, core: 2. Of those that a mesh axis runs over, the one named last changes fastest.
Arguments:
- values: bfloat16 [16384, 4096], P('tm', 'chan'), may hold values from -6 to 6
- gates: bfloat16 [16384, 4096], P('tm', 'chan'), may hold values from -6 to 6
- cotangent: bfloat16 [16384, 4096], P('tm', 'chan'), may hold values from -6 to 6
- kernel_taps: bfloat16 [256, 4096], P(None, 'chan'), may hold values from -0.375 to 0.375
- value_weight: bfloat16 [4096, 4096], P('tm', 'chan'), may hold values from -0.09375 to 0.09375
- gate_weight: bfloat16 [4096, 4096], P('tm', 'chan'), may hold values from -0.09375 to 0.09375
Outputs:
- grad_input: bfloat16 [16384, 4096], P('tm', 'chan')
- kernel_grad: float32 [256, 4096], P('tm', 'chan')
All inputs are finite; a program needn't handle non-finite values.
Results may differ from a plain program's by a relative error of at most 0.017.
Values may be sent and summed in bfloat16 or wider, within the bound.
A program may use at most 64 MiB of HBM per device.

v0:
```python
import math

import jax
import jax.numpy as jnp
import numpy as np
from jax import lax
from jax.sharding import PartitionSpec as P


def from_behind(value, axis, steps):
    count = lax.axis_size(axis)
    initial, last = (max(0, -steps), min(count, count - steps))
    return lax.ppermute(value, axis, [(source, source + steps) for source in range(initial, last)])


def contract_rows(left, weight_rows):
    return lax.dot_general(
        left, weight_rows, (((1,), (1,)), ((), ())), preferred_element_type=jnp.float32
    )


def forward_tables(length):
    freq_count = length // 2 + 1
    phase = np.arange(freq_count)[:, None] * np.arange(length)[None, :] % length
    angle = phase * (2.0 * np.pi / length)
    return (
        jnp.asarray(np.cos(angle), dtype=jnp.float32),
        jnp.asarray(np.sin(angle), dtype=jnp.float32),
    )


def inverse_tables(first, count, length):
    freq_count = length // 2 + 1
    freqs = np.arange(freq_count)
    phase = (first + np.arange(count))[:, None] * freqs[None, :] % length
    angle = phase * (2.0 * np.pi / length)
    weight = np.where((freqs == 0) | (freqs == length // 2), 1.0, 2.0) / length
    return (
        jnp.asarray(np.cos(angle) * weight[None, :], dtype=jnp.float32),
        jnp.asarray(np.sin(angle) * weight[None, :], dtype=jnp.float32),
    )


def precise_dot(left, right):
    return jnp.dot(left, right, precision=lax.Precision.HIGHEST, preferred_element_type=jnp.float32)


def back_to_time(first, count, length, real_part, imag_part):
    cos_inv, sin_inv = inverse_tables(first, count, length)
    return precise_dot(cos_inv, real_part) - precise_dot(sin_inv, imag_part)


def body(values, gates, cotangent, kernel_taps, value_weight, gate_weight):
    row_count, chan_count = values.shape
    span_len = kernel_taps.shape[0]
    window_len = row_count + span_len
    grad_conv = (cotangent.astype(jnp.float32) * gates.astype(jnp.float32)).astype(jnp.bfloat16)
    value_rim = from_behind(values[row_count - span_len + 1 :], "tm", 1)
    grad_rim = from_behind(grad_conv[: span_len - 1], "tm", -1)
    zero_row = jnp.zeros((1, chan_count), jnp.bfloat16)
    value_window = jnp.concatenate([zero_row, value_rim, values], 0)
    grad_window = jnp.concatenate([grad_conv, grad_rim, zero_row], 0)
    grad_padded = jnp.concatenate([jnp.zeros((span_len, chan_count), jnp.bfloat16), grad_conv], 0)
    taps_padded = jnp.concatenate(
        [kernel_taps, jnp.zeros((row_count, chan_count), jnp.bfloat16)], 0
    )
    joined_time = jnp.concatenate([value_window, grad_window, grad_padded, taps_padded], 1).astype(
        jnp.float32
    )
    cos_fwd, sin_fwd = forward_tables(window_len)
    real_all = precise_dot(cos_fwd, joined_time)
    imag_all = -precise_dot(sin_fwd, joined_time)
    value_re = real_all[:, :chan_count]
    value_im = imag_all[:, :chan_count]
    grad_re = real_all[:, chan_count : 2 * chan_count]
    grad_im = imag_all[:, chan_count : 2 * chan_count]
    pad_re = real_all[:, 2 * chan_count : 3 * chan_count]
    pad_im = imag_all[:, 2 * chan_count : 3 * chan_count]
    taps_re = real_all[:, 3 * chan_count :]
    taps_im = imag_all[:, 3 * chan_count :]
    conv_out = back_to_time(
        span_len,
        row_count,
        window_len,
        value_re * taps_re - value_im * taps_im,
        value_re * taps_im + value_im * taps_re,
    )
    grad_value = back_to_time(
        0,
        row_count,
        window_len,
        grad_re * taps_re + grad_im * taps_im,
        grad_im * taps_re - grad_re * taps_im,
    ).astype(jnp.bfloat16)
    norm_scale = 1.0 / math.sqrt(row_count * lax.axis_size("tm"))
    kernel_part = (
        back_to_time(
            0,
            span_len,
            window_len,
            pad_re * value_re + pad_im * value_im,
            pad_im * value_re - pad_re * value_im,
        )
        * norm_scale
    )
    grad_gate = (cotangent.astype(jnp.float32) * conv_out).astype(jnp.bfloat16)
    kernel_grad = lax.psum_scatter(kernel_part, "tm", scatter_dimension=0, tiled=True)
    terms = contract_rows(grad_value, lax.all_gather(value_weight, "tm", axis=0, tiled=True))
    terms = terms + contract_rows(grad_gate, lax.all_gather(gate_weight, "tm", axis=0, tiled=True))
    grad_input = lax.psum_scatter(
        terms.astype(jnp.bfloat16), "chan", scatter_dimension=1, tiled=True
    )
    return (grad_input, kernel_grad)


def solution(mesh):
    placed = (
        P("tm", "chan"),
        P("tm", "chan"),
        P("tm", "chan"),
        P(None, "chan"),
        P("tm", "chan"),
        P("tm", "chan"),
    )
    return jax.shard_map(
        body,
        mesh=mesh,
        in_specs=placed,
        out_specs=(P("tm", "chan"), P("tm", "chan")),
        check_vma=False,
    )
```

profile of v0, /device:TPU:1, one launch (start us, length us, event | category | flops | bytes accessed | tf_op | source)
XLA Modules:
  0.0 390.2 jit_solution(17819899406508750567)
XLA Ops:
  7.2 0.0 all-gather.3.cloned.1.call-start
  7.2 0.7 all-gather.3.cloned.1.call-update
  7.9 0.0 all-gather.5.cloned.1.call-start
  7.9 0.7 all-gather.5.cloned.1.call-update
  8.6 0.0 all-reduce.5.cloned.1.call-start
  8.7 1.0 slice.30
  9.7 0.0 copy-start.5
  9.7 4.2 %collective-permute-start = (bf16[255,512]{1,0:T(8,128)(2,1)S(1)}, bf16[255,512]{1,0:T(8,128)(2,1)S(1)}, u32[]{:S(2)}, u32[]{:S(2)}) collective-permute-start(bf16[255,512]{1,0:T(8,128)(2,1)S(1)} %slice.30), channel_id=1, source_target_pairs={{0,8},{8,16},{16,24},{24,32},{32,40},{40,48},{48,56},{56,64},{64,7... | collective-permute-start | bytes 783368 | tf_op jit(solution)/shard_map/ppermute | solution.py:13
  13.9 1.1 fusion.34
  15.0 1.3 collective-permute-start.1
  16.3 0.9 collective-permute-done
  17.2 4.9 %collective-permute-done.1 = bf16[255,512]{1,0:T(8,128)(2,1)S(1)} collective-permute-done((bf16[255,512]{1,0:T(8,128)(2,1)S(1)}, bf16[255,512]{1,0:T(8,128)(2,1)S(1)}, u32[]{:S(2)}, u32[]{:S(2)}) %collective-permute-start.1) | collective-permute-done | bytes 261152 | tf_op jit(solution)/shard_map/ppermute | solution.py:13
  22.1 4.9 %fusion.6 = bf16[512,2048]{1,0:T(8,128)(2,1)S(1)} fusion(bf16[256,512]{1,0:T(8,128)(2,1)} %param.17, bf16[256,512]{1,0:T(8,128)(2,1)S(1)} %fusion.34, bf16[1,512]{1,0:T(2,128)(2,1)S(1)} %broadcast_in_dim.3, bf16[255,512]{1,0:T(8,128)(2,1)S(1)} %collective-permute-done.1, bf16[256,512]{1,0:T(8,128)(2,1)} %param.14, bf16[255,512]{1,0:T(8,128)(2,1)S(1)} %collective-permute-done), kind=kLoop, calls=%fused_computation.11 | loop fusion | flops 23068672 | bytes 3406848 | tf_op jit(solution)/shard_map/concatenate | solution.py:67
  27.0 0.0 copy-done.5
  27.0 0.0 copy-start.3
  27.0 1.9 fusion.4
  28.9 0.0 copy-done.3
  28.9 0.0 copy-start
  28.9 0.0 copy-start.2
  28.9 1.9 fusion.59
  30.8 0.0 copy-done.2
  30.8 0.0 copy-start.6
  30.8 1.5 fusion.16
  32.3 0.0 copy-start.1
  32.3 1.5 fusion.30
  33.8 0.0 copy-done.6
  33.8 1.1 fusion.23
  35.0 0.0 copy-done.1
  35.0 0.0 copy-start.4
  35.0 1.5 fusion.12
  36.5 0.0 copy-done
  36.5 2.3 fusion.8
  38.8 0.0 all-reduce.5.cloned.1.call-update
  38.8 0.3 reduce-scatter.3.cloned.1.call-start
  39.1 0.0 copy-done.4
  39.1 2.4 fusion.11
  41.6 58.3 %all-gather.3.cloned.1.call-done = bf16[4096,512]{1,0:T(8,128)(2,1)} async-done(((bf16[64,512]{1,0:T(8,128)(2,1)}), bf16[4096,512]{1,0:T(8,128)(2,1)}) %all-gather.3.cloned.1.call-update) | async-done | bytes 4194320 | tf_op jit(solution)/shard_map/all_gather | solution.py:108
  99.8 5.5 %fusion.60 = f32[256,4096]{1,0:T(8,128)} fusion(bf16[512,256]{1,0:T(8,128)(2,1)S(1)} %fusion.12, bf16[4096,512]{1,0:T(8,128)(2,1)} %all-gather.3.cloned.1.call-done), kind=kOutput, calls=%fused_computation.70 | convolution fusion | flops 1073741824 | bytes 8650752 | tf_op jit(solution)/shard_map/dot_general | solution.py:17
  105.3 81.5 %all-gather.5.cloned.1.call-done = bf16[4096,512]{1,0:T(8,128)(2,1)} async-done(((bf16[64,512]{1,0:T(8,128)(2,1)}), bf16[4096,512]{1,0:T(8,128)(2,1)}) %all-gather.5.cloned.1.call-update) | async-done | bytes 4194320 | tf_op jit(solution)/shard_map/all_gather | solution.py:109
  186.7 6.1 %fusion = bf16[256,4096]{1,0:T(8,128)(2,1)} fusion(f32[256,4096]{1,0:T(8,128)} %fusion.60, bf16[256,512]{1,0:T(8,128)(2,1)S(1)} %fusion.11, bf16[4096,512]{1,0:T(8,128)(2,1)} %all-gather.5.cloned.1.call-done), kind=kOutput, calls=%fused_computation.3 | convolution fusion | flops 1075838976 | bytes 10747904 | tf_op jit(solution)/shard_map/dot_general | solution.py:17
  192.8 0.0 reduce-scatter.3.cloned.1.call-update
  192.9 1.3 dynamic-slice
  194.8 147.5 %all-reduce.5.cloned.1.call-done = f32[256,512]{0,1:T(8,128)} async-done(((f32[256,512]{0,1:T(8,128)}), f32[256,512]{0,1:T(8,128)}) %all-reduce.5.cloned.1.call-update) | async-done | bytes 524304
  342.3 1.1 constant_dynamic-slice_fusion
  343.4 0.7 copy.17
  344.1 39.6 %reduce-scatter.3.cloned.1.call-done = bf16[256,512]{1,0:T(8,128)(2,1)} async-done(((bf16[256,4096]{1,0:T(8,128)(2,1)}), bf16[256,512]{1,0:T(8,128)(2,1)}) %reduce-scatter.3.cloned.1.call-update) | async-done | bytes 262160 | tf_op jit(solution)/shard_map/reduce_scatter | solution.py:110
  (1 shorter events, 0.0 us)
Async XLA Ops:
  7.2 92.6 %all-gather.3.cloned.1.call-start = ((), (), s32[]{:S(2)}) async-start(), calls=%async_computation.1 | async-start | bytes 4259840 | tf_op jit(solution)/shard_map/all_gather | solution.py:108
  7.9 178.8 %all-gather.5.cloned.1.call-start = ((), (), s32[]{:S(2)}) async-start(), calls=%async_computation.2 | async-start | bytes 4259840 | tf_op jit(solution)/shard_map/all_gather | solution.py:109
  8.6 333.7 %all-reduce.5.cloned.1.call-start = ((), (), s32[]{:S(2)}) async-start(), calls=%async_computation.4 | async-start | bytes 1048576
  9.7 17.3 %copy-start.5 = (f32[257,512]{1,0:T(8,128)S(1)}, f32[257,512]{1,0:T(8,128)}, u32[]{:S(2)}) copy-start(f32[257,512]{1,0:T(8,128)} %constant.18.clone) | copy-start | bytes 1579012
  9.7 7.5 %collective-permute-start = (bf16[255,512]{1,0:T(8,128)(2,1)S(1)}, bf16[255,512]{1,0:T(8,128)(2,1)S(1)}, u32[]{:S(2)}, u32[]{:S(2)}) collective-permute-start(bf16[255,512]{1,0:T(8,128)(2,1)S(1)} %slice.30), channel_id=1, source_target_pairs={{0,8},{8,16},{16,24},{24,32},{32,40},{40,48},{48,56},{56,64},{64,7... | collective-permute-start | bytes 783368 | tf_op jit(solution)/shard_map/ppermute | solution.py:13
  15.0 7.1 %collective-permute-start.1 = (bf16[255,512]{1,0:T(8,128)(2,1)S(1)}, bf16[255,512]{1,0:T(8,128)(2,1)S(1)}, u32[]{:S(2)}, u32[]{:S(2)}) collective-permute-start(bf16[255,512]{1,0:T(8,128)(2,1)S(1)} %bitcast.28), channel_id=1, source_target_pairs={{8,0},{16,8},{24,16},{32,24},{40,32},{48,40},{56,48},{64,56},{72,6... | collective-permute-start | bytes 783368 | tf_op jit(solution)/shard_map/ppermute | solution.py:13
  27.0 1.9 copy-start.3
  28.9 7.6 %copy-start = (f32[257,2048]{1,0:T(8,128)}, f32[257,2048]{1,0:T(8,128)S(1)}, u32[]{:S(2)}) copy-start(f32[257,2048]{1,0:T(8,128)S(1)} %fusion.4) | copy-start | bytes 6316036
  28.9 1.9 copy-start.2
  30.8 3.0 copy-start.6
  32.3 2.6 copy-start.1
  35.0 4.1 %copy-start.4 = (bf16[256,512]{1,0:T(8,128)(2,1)S(1)}, bf16[256,512]{1,0:T(8,128)(2,1)}, u32[]{:S(2)}) copy-start(bf16[256,512]{1,0:T(8,128)(2,1)} %param.16) | copy-start | bytes 786436
  38.8 344.8 %reduce-scatter.3.cloned.1.call-start = ((), (), s32[]{:S(2)}) async-start(), calls=%async_computation.3 | async-start | bytes 2359296 | tf_op jit(solution)/shard_map/reduce_scatter | solution.py:110
Sparse Core Ops, SparseCore 0:
  11.1 88.7 all-gather.2
  102.9 83.8 all-gather.4
  190.0 152.3 all-reduce.4
  345.8 37.7 reduce-scatter.2
where the time goes:
time: 391 us; the launch traced here: 390 us
  waiting for transfers between devices  334 us (85%)
  matrix products  25.6 us (7%)
  between operations  14.6 us (4%)
  other arithmetic  5.97 us (2%)
  starting transfers between devices  5.85 us (1%)
  local copies, waits for them, and re-layouts  4.12 us (1%)
    unnamed x5, waiting for transfers between devices  149 us
    all_gather x1, waiting for transfers between devices, body(): lax.all_gather(gate_weight, 'tm', axis=0, tiled=True)  81.5 us
    all_gather x1, waiting for transfers between devices, body(): lax.all_gather(value_weight, 'tm', axis=0, tiled=True)  58.3 us
    reduce_scatter x1, waiting for transfers between devices, body(): lax.psum_scatter(terms.astype(jnp.bfloat16), 'chan', scatter_dimension=1,...  39.6 us
    dot_general x8, matrix products, precise_dot(): jnp.dot(left, right, precision=lax.Precision.HIGHEST, preferred_element_t...  14.1 us
    dot_general x2, matrix products, contract_rows(): lax.dot_general(left, weight_rows, (((1,), (1,)), ((), ())), preferred_el...  11.6 us
  transfers between devices with their start and end apart: 6, of which 6 were waited for; matrix products, arithmetic and copies ran while one was open for 9% of the time, Pallas kernels for 0%

commit v1 on v0

v1 whole, which is shorter than its diff:
```python
import functools
import math

import jax
import jax.numpy as jnp
import ml_dtypes
import numpy as np
from jax import lax
from jax.experimental import pallas as pl
from jax.experimental.pallas import tpu as pltpu
from jax.sharding import PartitionSpec as P

MESH = pl.DeviceIdType.MESH
BF16 = jnp.bfloat16
F32 = jnp.float32
RING = 8
SLOT = {0: 0, -1: 1, 1: 2, -2: 3, 2: 4, -3: 5, 3: 6, 4: 7}


def split_table(table):
    high = table.astype(ml_dtypes.bfloat16)
    low = (table - high.astype(np.float64)).astype(ml_dtypes.bfloat16)
    return jnp.asarray(high), jnp.asarray(low)


def dft_tables(half):
    length = 2 * half
    step = np.arange(length)
    freq = np.arange(half)
    angle = (freq[:, None] * step[None, :] % length) * (2.0 * np.pi / length)
    cosine, sine = np.cos(angle), -np.sin(angle)
    sine[0] = np.where(step % 2 == 0, 1.0, -1.0)
    forward = np.concatenate([cosine, sine], 0)
    weight = np.full((length,), 2.0 / length)
    weight[0] = weight[half] = 1.0 / length
    inverse = (forward[:, :half] * weight[:, None]).T
    return forward, inverse


def wrap(index):
    return lax.rem(index + RING, RING)


def slot_of(distance):
    far = lax.div(distance, 4)
    return (1 - far) * 2 * distance + far * (15 - 2 * distance)


def mm(left, right):
    return jnp.dot(left, right, preferred_element_type=F32)


def kernel(
    norm_scale,
    values,
    gates,
    cotangent,
    taps,
    value_weight,
    gate_weight,
    fwd_hi,
    fwd_lo,
    inv_hi,
    inv_lo,
    out,
    kernel_grad,
    gather_a,
    gather_b,
    value_rim,
    grad_win,
    spec_v,
    spec_g,
    spec_p,
    spec_t,
    prod_hi,
    prod_lo,
    left_v,
    left_g,
    part_a,
    part_b,
    got_a,
    got_b,
    kz_send,
    kz_got,
    ky_send,
    ky_got,
    rim_send_sem,
    rim_recv_sem,
    p1_send,
    p1_recv,
    p2_send,
    p2_recv,
    a_send,
    a_recv,
    b_send,
    b_recv,
    kz_send_sem,
    kz_recv_sem,
    ky_send_sem,
    ky_recv_sem,
):
    rows = values.shape[0]
    tm = lax.axis_index("tm")
    me = lax.axis_index("chan")
    z, y = lax.div(tm, RING), lax.rem(tm, RING)

    def at_y(distance):
        return z * RING + wrap(y + distance)

    def at_z(distance):
        return wrap(z + distance) * RING + y

    def remote(src, dst, send_sem, recv_sem, axis, index):
        return pltpu.make_async_remote_copy(
            src_ref=src,
            dst_ref=dst,
            send_sem=send_sem,
            recv_sem=recv_sem,
            device_id={axis: index},
            device_id_type=MESH,
        )

    barrier = pltpu.get_barrier_semaphore()

    def greet(axis, index):
        pl.semaphore_signal(barrier, inc=1, device_id={axis: index}, device_id_type=MESH)

    for distance in range(1, RING):
        greet("tm", at_y(distance))
        greet("tm", at_z(distance))
        greet("chan", wrap(me + distance))
    after = lax.rem(tm + 1, RING * RING)
    before = lax.rem(tm + RING * RING - 1, RING * RING)
    greet("tm", after)
    greet("tm", before)

    half = value_weight.shape[0] // 2
    for which, weight in ((0, value_weight), (1, gate_weight)):
        gather_a[0, 0, which] = weight[:half]
        gather_b[0, 0, which] = weight[half:]
    grad_win[:rows] = (cotangent[...].astype(F32) * gates[...].astype(F32)).astype(BF16)

    pl.semaphore_wait(barrier, 3 * (RING - 1) + 2)

    sends = []

    def go(copy):
        copy.start()
        sends.append(copy)
        return copy

    rim_v = go(remote(values, value_rim, rim_send_sem.at[0], rim_recv_sem.at[0], "tm", after))
    rim_g = go(
        remote(
            grad_win.at[:rows], grad_win.at[rows:], rim_send_sem.at[1], rim_recv_sem.at[1], "tm", before
        )
    )

    buffers = (gather_a, gather_b)
    first_axis = (at_y, at_z)
    second_axis = (at_z, at_y)
    stage1, stage2 = {}, {}

    def send1(color, way, distance):
        sign = -1 if way == 0 else 1
        src = buffers[color].at[0, SLOT[sign * distance]]
        if distance < 3:
            dst = buffers[color].at[0, SLOT[sign * (distance + 1)]]
        else:
            src, dst = src.at[way], buffers[color].at[0, SLOT[4], way]
        stage1[color, way, distance] = go(
            remote(
                src,
                dst,
                p1_send.at[color, way, distance],
                p1_recv.at[color, way, distance],
                "tm",
                first_axis[color](-sign),
            )
        )

    def send2(color, way, distance, part):
        sign = -1 if way == 0 else 1
        blocks = pl.ds(4 * part, 4)
        src = buffers[color].at[SLOT[sign * distance], blocks]
        target = SLOT[4] if distance == 3 else SLOT[sign * (distance + 1)]
        dst = buffers[color].at[target, blocks]
        at = 6 if distance == 3 else 2 * distance + part
        stage2[color, way, distance, part] = go(
            remote(
                src,
                dst,
                p2_send.at[color, way, at],
                p2_recv.at[color, way, at],
                "tm",
                second_axis[color](-sign),
            )
        )

    pairs = [(color, way) for way in (0, 1) for color in (0, 1)]

    def serve1(distance):
        for color, way in pairs:
            stage1[color, way, distance - 1].wait_recv()
            if distance < 4:
                send1(color, way, distance)

    def start2(part):
        for color, way in pairs:
            send2(color, way, 0, part)

    def serve2(distance, part):
        for color, way in pairs:
            stage2[color, way, distance - 1, part].wait_recv()
            if distance < 3 or part == way:
                send2(color, way, distance, part)

    for color, way in pairs:
        send1(color, way, 0)

    def forward(first, data):
        cols = slice(0, rows) if first else slice(rows, 2 * rows)
        return mm(fwd_hi[:, cols], data) + mm(fwd_lo[:, cols], data)

    spec_t[...] = forward(True, taps[...])
    serve1(1)
    spec_p[...] = forward(True, grad_win[:rows])
    serve1(2)
    start2(0)
    spec_v[...] = forward(False, values[...])
    serve1(3)
    rim_v.wait_recv()
    has_before = (tm > 0).astype(F32)
    spec_v[...] = spec_v[...] + forward(True, value_rim[...]) * has_before
    rim_g.wait_recv()
    has_after = (tm < RING * RING - 1).astype(F32)
    spec_g[...] = spec_p[...] + forward(False, grad_win[rows:]) * has_after
    serve1(4)
    start2(1)

    chans = values.shape[1]
    width = 128
    row_at = lax.broadcasted_iota(jnp.int32, (rows, width), 0)
    first_row = row_at == 0
    sign = (1 - 2 * (row_at & 1)).astype(F32)

    def product(left_re, left_im, right_re, right_im, flip):
        cross = left_im * right_im
        real = left_re * right_re
        if flip:
            imag = left_im * right_re - left_re * right_im
            real = real + jnp.where(first_row, 0.0, cross)
        else:
            imag = left_im * right_re + left_re * right_im
            real = real - jnp.where(first_row, 0.0, cross)
        return real, jnp.where(first_row, cross, imag)

    def keep(real, imag, at):
        for part, data in ((slice(0, rows), real), (slice(rows, 2 * rows), imag)):
            high = data.astype(BF16)
            prod_hi[part, at : at + width] = high
            prod_lo[part, at : at + width] = (data - high.astype(F32)).astype(BF16)

    for col in range(0, chans, width):
        cut = slice(col, col + width)
        v_re, v_im = spec_v[:rows, cut], spec_v[rows:, cut]
        t_re, t_im = spec_t[:rows, cut], spec_t[rows:, cut]
        g_re, g_im = spec_g[:rows, cut], spec_g[rows:, cut]
        p_re, p_im = spec_p[:rows, cut] * sign, spec_p[rows:, cut] * sign
        real, imag = product(v_re, v_im, t_re, t_im, False)
        keep(real * sign, imag * sign, col)
        real, imag = product(g_re, g_im, t_re, t_im, True)
        keep(real, imag, chans + col)
        real, imag = product(p_re, p_im, v_re, v_im, True)
        keep(real, imag, 2 * chans + col)

    def backward(index):
        cut = slice(index * chans, (index + 1) * chans)
        return (
            mm(inv_hi[...], prod_hi[:, cut])
            + mm(inv_hi[...], prod_lo[:, cut])
            + mm(inv_lo[...], prod_hi[:, cut])
        )

    partial_kernel = backward(2) * norm_scale
    kz_send[...] = partial_kernel.reshape(kz_send.shape).astype(BF16)
    kz = []
    for distance in range(1, RING):
        kz.append(
            go(
                remote(
                    kz_send.at[wrap(z + distance)],
                    kz_got.at[RING - distance],
                    kz_send_sem.at[RING - distance],
                    kz_recv_sem.at[RING - distance],
                    "tm",
                    at_z(distance),
                )
            )
        )
    serve2(1, 0)
    left_v[...] = backward(1).T.astype(BF16)
    left_g[...] = (cotangent[...].astype(F32) * backward(0)).T.astype(BF16)

    def multiply(color, slots, blocks):
        ref = buffers[color]
        count = (slots[1] - slots[0]) * (blocks[1] - blocks[0]) * half
        total = mm(
            ref[slots[0] : slots[1], blocks[0] : blocks[1], 0].reshape(count, chans), left_v[...]
        )
        total = total + mm(
            ref[slots[0] : slots[1], blocks[0] : blocks[1], 1].reshape(count, chans), left_g[...]
        )
        total = total.astype(BF16)
        for slot in range(slots[0], slots[1]):
            for block in range(blocks[0], blocks[1]):
                at = ((slot - slots[0]) * (blocks[1] - blocks[0]) + block - blocks[0]) * half
                if color == 0:
                    part_a[slot, block] = total[at : at + half]
                else:
                    part_b[block, slot] = total[at : at + half]

    places = {slot: place for place, slot in SLOT.items()}

    def copy_a(slot, part):
        owner = wrap(z + places[slot])
        blocks = pl.ds(4 * part, 4)
        at = wrap(me - owner)
        return owner, remote(
            part_a.at[slot, blocks],
            got_a.at[at, blocks],
            a_send.at[slot, part],
            a_recv.at[at, part],
            "chan",
            owner,
        )

    sent_a = []

    def give_a(slot, part):
        owner, copy = copy_a(slot, part)
        sent_a.append((slot, part))

        @pl.when(owner != me)
        def _():
            copy.start()

    def give_b(group, slots):
        for distance in range(1, RING):
            owner = wrap(me + distance)
            row = slot_of(wrap(owner - z))
            go(
                remote(
                    part_b.at[row, slots],
                    got_b.at[RING - distance, slots],
                    b_send.at[group, RING - distance],
                    b_recv.at[group, RING - distance],
                    "chan",
                    owner,
                )
            )

    multiply(0, (0, 1), (0, 8))
    give_a(0, 0)
    give_a(0, 1)
    multiply(1, (0, 1), (0, 8))
    give_b(0, pl.ds(0, 1))

    ky = []
    for distance in (1, 2, 3):
        slots = (2 * distance - 1, 2 * distance + 1)
        for part in (0, 1):
            if (distance, part) != (1, 0):
                serve2(distance, part)
            for color in (0, 1):
                multiply(color, slots, (4 * part, 4 * part + 4))
                if color == 0:
                    give_a(slots[0], part)
                    give_a(slots[0] + 1, part)
        give_b(distance, pl.ds(slots[0], 2))
        if distance == 1:
            for copy in kz:
                copy.wait_recv()
            total = kz_send[z].astype(F32)
            for index in range(1, RING):
                total = total + kz_got[index].astype(F32)
            lags = ky_send.shape[1]
            for index in range(RING):
                ky_send[index] = total[index * lags : (index + 1) * lags]
            for index in range(1, RING):
                ky.append(
                    go(
                        remote(
                            ky_send.at[wrap(y + index)],
                            ky_got.at[RING - index],
                            ky_send_sem.at[RING - index],
                            ky_recv_sem.at[RING - index],
                            "tm",
                            at_y(index),
                        )
                    )
                )
        if distance == 2:
            for copy in ky:
                copy.wait_recv()
            total = ky_send[y]
            for index in range(1, RING):
                total = total + ky_got[index]
            kernel_grad[...] = total

    for color, way in pairs:
        stage2[color, way, 3, way].wait_recv()
    multiply(0, (7, 8), (0, 8))
    give_a(7, 0)
    give_a(7, 1)
    multiply(1, (7, 8), (0, 8))
    give_b(4, pl.ds(7, 1))

    for index in range(1, RING):
        for part in (0, 1):
            blocks = pl.ds(4 * part, 4)
            remote(
                part_a.at[0, blocks],
                got_a.at[index, blocks],
                a_send.at[0, part],
                a_recv.at[index, part],
                "chan",
                wrap(me + index),
            ).wait_recv()
        for group in range(5):
            slots = pl.ds(0, 1) if group == 0 else pl.ds(2 * group - 1, 1 if group == 4 else 2)
            remote(
                part_b.at[0, slots],
                got_b.at[index, slots],
                b_send.at[group, index],
                b_recv.at[group, index],
                "chan",
                wrap(me + index),
            ).wait_recv()

    own = slot_of(wrap(me - z))
    for pair in range(RING // 2):
        pieces = []
        for place in (2 * pair, 2 * pair + 1):
            block = slot_of(wrap(place - y))
            for part, got in ((part_a, got_a), (part_b, got_b)):
                total = part[own, block].astype(F32)
                for index in range(1, RING):
                    total = total + got[index, block].astype(F32)
                pieces.append(total)
        merged = jnp.concatenate(pieces, 0)
        out[:, 4 * half * pair : 4 * half * (pair + 1)] = merged.T.astype(BF16)

    for copy in sends:
        copy.wait_send()
    for slot, part in sent_a:
        owner, copy = copy_a(slot, part)

        @pl.when(owner != me)
        def _():
            copy.wait_send()


def body(norm_scale, tables, *args):
    values, _, _, taps, value_weight, _ = args
    rows, chans = values.shape
    half = value_weight.shape[0] // 2
    lags = taps.shape[0] // (RING * RING)
    assert taps.shape[0] == rows and lax.axis_size("tm") == RING * RING
    assert lax.axis_size("chan") == RING and chans == RING * 2 * half
    vmem = pl.BlockSpec(memory_space=pltpu.VMEM)
    dma = pltpu.SemaphoreType.DMA
    return pl.pallas_call(
        functools.partial(kernel, norm_scale),
        out_shape=(
            jax.ShapeDtypeStruct((rows, chans), BF16),
            jax.ShapeDtypeStruct((lags, chans), F32),
        ),
        in_specs=[vmem] * 10,
        out_specs=(vmem, vmem),
        scratch_shapes=[
            pltpu.VMEM((RING, RING, 2, half, chans), BF16),
            pltpu.VMEM((RING, RING, 2, half, chans), BF16),
            pltpu.VMEM((rows, chans), BF16),
            pltpu.VMEM((2 * rows, chans), BF16),
            pltpu.VMEM((2 * rows, chans), F32),
            pltpu.VMEM((2 * rows, chans), F32),
            pltpu.VMEM((2 * rows, chans), F32),
            pltpu.VMEM((2 * rows, chans), F32),
            pltpu.VMEM((2 * rows, 3 * chans), BF16),
            pltpu.VMEM((2 * rows, 3 * chans), BF16),
            pltpu.VMEM((chans, rows), BF16),
            pltpu.VMEM((chans, rows), BF16),
            pltpu.VMEM((RING, RING, half, rows), BF16),
            pltpu.VMEM((RING, RING, half, rows), BF16),
            pltpu.VMEM((RING, RING, half, rows), BF16),
            pltpu.VMEM((RING, RING, half, rows), BF16),
            pltpu.VMEM((RING, RING * lags, chans), BF16),
            pltpu.VMEM((RING, RING * lags, chans), BF16),
            pltpu.VMEM((RING, lags, chans), F32),
            pltpu.VMEM((RING, lags, chans), F32),
            dma((2,)),
            dma((2,)),
            dma((2, 2, 4)),
            dma((2, 2, 4)),
            dma((2, 2, 7)),
            dma((2, 2, 7)),
            dma((RING, 2)),
            dma((RING, 2)),
            dma((5, RING)),
            dma((5, RING)),
            dma((RING,)),
            dma((RING,)),
            dma((RING,)),
            dma((RING,)),
        ],
        compiler_params=pltpu.CompilerParams(
            collective_id=0, has_side_effects=True, vmem_limit_bytes=56 * 1024 * 1024
        ),
    )(*args, *tables)


def solution(mesh):
    placed = (
        P("tm", "chan"),
        P("tm", "chan"),
        P("tm", "chan"),
        P(None, "chan"),
        P("tm", "chan"),
        P("tm", "chan"),
    )

    def program(values, gates, cotangent, kernel_taps, value_weight, gate_weight):
        fwd, inv = dft_tables(kernel_taps.shape[0])
        tables = (*split_table(fwd), *split_table(inv))
        norm_scale = 1.0 / math.sqrt(values.shape[0])
        return jax.shard_map(
            lambda *args: body(norm_scale, args[6:], *args[:6]),
            mesh=mesh,
            in_specs=placed + (P(),) * 4,
            out_specs=(P("tm", "chan"), P("tm", "chan")),
            check_vma=False,
        )(values, gates, cotangent, kernel_taps, value_weight, gate_weight, *tables)

    return program
```

time: 391 us -> 92.7 us (0.24)
  waiting for transfers between devices: 334 us -> 0 us
  Pallas kernels: 0 us -> 89.6 us
  matrix products: 25.6 us -> 0 us
  between operations: 14.6 us -> 0.65 us
  other arithmetic: 5.97 us -> 0 us
  starting transfers between devices: 5.85 us -> 0 us
    unnamed x5 -> x0, waiting for transfers between devices: 149 us -> none
    all_gather x2 -> x0, waiting for transfers between devices: 140 us -> none  [the longest x1 81.5 us: body(): lax.all_gather(gate_weight, 'tm', axis=0, tiled=True)]
    pallas_call x0 -> x1, Pallas kernels: none -> 89.6 us  [body(): pl.pallas_call(functools.partial(kernel, norm_scale), out_shape=(jax.Shap...]
    reduce_scatter x1 -> x0, waiting for transfers between devices: 39.6 us -> none  [body(): lax.psum_scatter(terms.astype(jnp.bfloat16), 'chan', scatter_dimension=1,...]
    dot_general x10 -> x0, matrix products: 25.6 us -> none  [the longest x8 14.1 us: precise_dot(): jnp.dot(left, right, precision=lax.Precision.HIGHEST, preferred_element_t...]
    ppermute x2 -> x0, waiting for transfers between devices: 5.82 us -> none  [from_behind(): lax.ppermute(value, axis, [(source, source + steps) for source in range(i...]
    ppermute x2 -> x0, starting transfers between devices: 5.47 us -> none  [from_behind(): lax.ppermute(value, axis, [(source, source + steps) for source in range(i...]
    concatenate x1 -> x0, other arithmetic: 4.87 us -> none  [body(): jnp.concatenate([value_window, grad_window, grad_padded, taps_padded], 1)]
  transfers between devices with their start and end apart: 6 -> 0, of which waited for: 6 -> 0; matrix products, arithmetic and copies ran while one was open for 9% -> 0% of each run, Pallas kernels for 0% -> 0%
where the time goes in v1:
time: 92.7 us; the launch traced here: 92.5 us
  Pallas kernels  89.6 us (97%)
  local copies, waits for them, and re-layouts  2.28 us (2%)
    pallas_call x1, Pallas kernels, body(): pl.pallas_call(functools.partial(kernel, norm_scale), out_shape=(jax.Shap...  89.6 us
    unnamed x4, local copies, waits for them, and re-layouts  2.28 us

profile of v1, /device:TPU:1, one launch (start us, length us, event | category | flops | bytes accessed | tf_op | source)
XLA Modules:
  0.0 92.5 jit_solution(17750404925594385443)
XLA Ops:
  0.6 89.6 %shard_map.113 = (bf16[256,512]{1,0:T(8,128)(2,1)}, f32[4,512]{1,0:T(4,128)}) custom-call(bf16[256,512]{1,0:T(8,128)(2,1)} %values.1, bf16[256,512]{1,0:T(8,128)(2,1)} %gates.1, bf16[256,512]{1,0:T(8,128)(2,1)} %cotangent.1, bf16[256,512]{1,0:T(8,128)(2,1)} %taps.1, bf16[64,512]{1,0:T(8,128)(2,1)} %value_weight.1, bf16[64,512]{1,0:T(8,128)(2,1)} %gate_weight.1, ...), custom_call_target="tpu_custom_call" | custom-call | tf_op jit(solution)/shard_map/pallas_call | solution.py:473
  90.2 0.0 copy-start
  90.2 1.7 %copy.14 = bf16[256,512]{1,0:T(8,128)(2,1)} copy(bf16[256,512]{1,0:T(8,128)(2,1)} %get-tuple-element.4) | data formatting | bytes 524288
  91.9 0.0 copy-done
  91.9 0.6 copy.15
Async XLA Ops:
  90.2 1.7 %copy-start = (f32[4,512]{1,0:T(4,128)S(1)}, f32[4,512]{1,0:T(4,128)}, u32[]{:S(2)}) copy-start(f32[4,512]{1,0:T(4,128)} %get-tuple-element.5) | copy-start | bytes 24580

commit v2 on v1

v2 whole, which is shorter than its diff:
```python
import functools
import math

import jax
import jax.numpy as jnp
import ml_dtypes
import numpy as np
from jax import lax
from jax.experimental import pallas as pl
from jax.experimental.pallas import tpu as pltpu
from jax.sharding import PartitionSpec as P

MESH = pl.DeviceIdType.MESH
BF16 = jnp.bfloat16
F32 = jnp.float32
RING = 8
SLOT = {0: 0, -1: 1, 1: 2, -2: 3, 2: 4, -3: 5, 3: 6, 4: 7}
GROUPS = ((0, 1), (1, 3), (3, 5), (5, 7), (7, 8))
PARTS = ((0, 5), (5, 8))
UNITS = [(color, slots, blocks) for slots in GROUPS for blocks in PARTS for color in (0, 1)]


def arrivals():
    found = []
    for way in (0, 1):
        for color in (0, 1):
            found += [(1, color, way, distance, 0) for distance in range(1, 5)]
            for distance in range(1, 5):
                for group, (low, high) in enumerate(GROUPS):
                    if distance < 4 or max(low, 4 * way) < min(high, 4 * way + 4):
                        found.append((2, color, way, distance, group))
    return sorted(found, key=lambda event: (event[3] + event[4], event[0], event[3]))


EVENTS = arrivals()
CHORE_EVERY = 7


def split_table(table):
    high = table.astype(ml_dtypes.bfloat16)
    low = (table - high.astype(np.float64)).astype(ml_dtypes.bfloat16)
    return jnp.asarray(high), jnp.asarray(low)


def dft_tables(half):
    length = 2 * half
    step = np.arange(length)
    freq = np.arange(half)
    angle = (freq[:, None] * step[None, :] % length) * (2.0 * np.pi / length)
    cosine, sine = np.cos(angle), -np.sin(angle)
    sine[0] = np.where(step % 2 == 0, 1.0, -1.0)
    forward = np.concatenate([cosine, sine], 0)
    weight = np.full((length,), 2.0 / length)
    weight[0] = weight[half] = 1.0 / length
    inverse = (forward[:, :half] * weight[:, None]).T
    return forward, inverse


def wrap(index):
    return lax.rem(index + RING, RING)


def slot_of(distance):
    far = lax.div(distance, 4)
    return (1 - far) * 2 * distance + far * (15 - 2 * distance)


def mm(left, right):
    return jnp.dot(left, right, preferred_element_type=F32)


def kernel(
    norm_scale,
    values_in,
    gates_in,
    cotangent_in,
    taps_in,
    value_weight,
    gate_weight,
    fwd_hi_in,
    fwd_lo_in,
    inv_hi_in,
    inv_lo_in,
    out,
    kernel_grad,
    values,
    gates,
    cotangent,
    taps,
    fwd_hi,
    fwd_lo,
    inv_hi,
    inv_lo,
    gather_a,
    gather_b,
    value_rim,
    grad_win,
    spec_v,
    spec_g,
    spec_p,
    spec_t,
    prod_hi,
    prod_lo,
    left_v,
    left_g,
    part_a,
    part_b,
    sib_a,
    sib_b,
    got_a,
    got_b,
    lag_part,
    kz_send,
    kz_got,
    lag_row,
    ky_send,
    ky_got,
    local_sem,
    rim_send_sem,
    rim_recv_sem,
    p1_send,
    p1_recv,
    p2_send,
    p2_recv,
    sib_send,
    sib_recv,
    a_send,
    a_recv,
    b_send,
    b_recv,
    kz_send_sem,
    kz_recv_sem,
    ky_send_sem,
    ky_recv_sem,
):
    rows = values.shape[0]
    tm = lax.axis_index("tm")
    me = lax.axis_index("chan")
    z, y = lax.div(tm, RING), lax.rem(tm, RING)

    def at_y(distance):
        return z * RING + wrap(y + distance)

    def at_z(distance):
        return wrap(z + distance) * RING + y

    def remote(src, dst, send_sem, recv_sem, axis, index):
        return pltpu.make_async_remote_copy(
            src_ref=src,
            dst_ref=dst,
            send_sem=send_sem,
            recv_sem=recv_sem,
            device_id={axis: index},
            device_id_type=MESH,
        )

    barrier = pltpu.get_barrier_semaphore()

    def greet(axis, index):
        pl.semaphore_signal(barrier, inc=1, device_id={axis: index}, device_id_type=MESH)

    half = value_weight.shape[0] // 2
    loads = []

    def load(src, dst):
        copy = pltpu.make_async_copy(src, dst, local_sem.at[len(loads)])
        copy.start()
        loads.append(copy)
        return copy

    own_rows = [
        load(weight.at[pl.ds(half * color, half)], gather.at[0, 0, which])
        for color, gather in ((0, gather_a), (1, gather_b))
        for which, weight in ((0, value_weight), (1, gate_weight))
    ]
    for distance in range(1, RING):
        greet("chan", wrap(me + distance))
    for distance in (-1, 1):
        greet("tm", at_y(distance))
        greet("tm", at_z(distance))
    after = lax.rem(tm + 1, RING * RING)
    before = lax.rem(tm + RING * RING - 1, RING * RING)
    greet("tm", after)
    greet("tm", before)
    streams = [load(cotangent_in, cotangent), load(gates_in, gates), load(values_in, values)]
    ahead = [load(taps_in, taps), load(fwd_hi_in, fwd_hi), load(fwd_lo_in, fwd_lo)]
    later = [load(inv_hi_in, inv_hi), load(inv_lo_in, inv_lo)]

    pl.semaphore_wait(barrier, (RING - 1) + 6)
    for copy in own_rows:
        copy.wait()

    sends = []

    def go(copy):
        copy.start()
        sends.append(copy)
        return copy

    buffers = (gather_a, gather_b)
    first_axis = (at_y, at_z)
    second_axis = (at_z, at_y)
    flights = {}

    def send1(color, way, distance):
        sign = -1 if way == 0 else 1
        src = buffers[color].at[0, SLOT[sign * distance]]
        if distance < 3:
            dst = buffers[color].at[0, SLOT[sign * (distance + 1)]]
        else:
            src, dst = src.at[way], buffers[color].at[0, SLOT[4], way]
        flights[1, color, way, distance + 1, 0] = go(
            remote(
                src,
                dst,
                p1_send.at[color, way, distance],
                p1_recv.at[color, way, distance],
                "tm",
                first_axis[color](-sign),
            )
        )

    def send2(color, way, distance, group):
        sign = -1 if way == 0 else 1
        low, high = GROUPS[group]
        target, at = SLOT[4], 15 + group
        if distance < 3:
            target, at = SLOT[sign * (distance + 1)], 5 * distance + group
        else:
            low, high = max(low, 4 * way), min(high, 4 * way + 4)
            if low >= high:
                return
        blocks = pl.ds(low, high - low)
        flights[2, color, way, distance + 1, group] = go(
            remote(
                buffers[color].at[SLOT[sign * distance], blocks],
                buffers[color].at[target, blocks],
                p2_send.at[color, way, at],
                p2_recv.at[color, way, at],
                "tm",
                second_axis[color](-sign),
            )
        )

    pairs = [(color, way) for way in (0, 1) for color in (0, 1)]

    def serve(event):
        stage, color, way, distance, group = event
        flights[event].wait_recv()
        if stage == 1:
            if distance < 4:
                send1(color, way, distance)
            if way == 1:
                for out_way in (0, 1):
                    send2(color, out_way, 0, distance)
        elif distance < 4:
            send2(color, way, distance, group)

    for color, way in pairs:
        send1(color, way, 0)
        send2(color, way, 0, 0)

    for copy in streams:
        copy.wait()
    grad_win[:rows] = (cotangent[...].astype(F32) * gates[...].astype(F32)).astype(BF16)
    rim_v = go(remote(values, value_rim, rim_send_sem.at[0], rim_recv_sem.at[0], "tm", after))
    rim_g = go(
        remote(
            grad_win.at[:rows], grad_win.at[rows:], rim_send_sem.at[1], rim_recv_sem.at[1], "tm", before
        )
    )

    def forward(first, data):
        cols = slice(0, rows) if first else slice(rows, 2 * rows)
        return mm(fwd_hi[:, cols], data) + mm(fwd_lo[:, cols], data)

    steps = {}
    for event in EVENTS:
        steps.setdefault(event[3] + event[4], []).append(event)

    for copy in ahead:
        copy.wait()
    spec_t[...] = forward(True, taps[...])
    spec_p[...] = forward(True, grad_win[:rows])
    for event in steps[1]:
        serve(event)
    spec_v[...] = forward(False, values[...])
    for event in steps[2]:
        serve(event)
    rim_v.wait_recv()
    has_before = (tm > 0).astype(F32)
    spec_v[...] = spec_v[...] + forward(True, value_rim[...]) * has_before
    rim_g.wait_recv()
    has_after = (tm < RING * RING - 1).astype(F32)
    spec_g[...] = spec_p[...] + forward(False, grad_win[rows:]) * has_after

    chans = values.shape[1]
    width = 128
    row_at = lax.broadcasted_iota(jnp.int32, (rows, width), 0)
    first_row = row_at == 0
    sign = (1 - 2 * (row_at & 1)).astype(F32)

    def product(left_re, left_im, right_re, right_im, flip):
        cross = left_im * right_im
        real = left_re * right_re
        if flip:
            imag = left_im * right_re - left_re * right_im
            real = real + jnp.where(first_row, 0.0, cross)
        else:
            imag = left_im * right_re + left_re * right_im
            real = real - jnp.where(first_row, 0.0, cross)
        return real, jnp.where(first_row, cross, imag)

    def keep(real, imag, at):
        for part, data in ((slice(0, rows), real), (slice(rows, 2 * rows), imag)):
            high = data.astype(BF16)
            prod_hi[part, at : at + width] = high
            prod_lo[part, at : at + width] = (data - high.astype(F32)).astype(BF16)

    for col in range(0, chans, width):
        cut = slice(col, col + width)
        v_re, v_im = spec_v[:rows, cut], spec_v[rows:, cut]
        t_re, t_im = spec_t[:rows, cut], spec_t[rows:, cut]
        g_re, g_im = spec_g[:rows, cut], spec_g[rows:, cut]
        p_re, p_im = spec_p[:rows, cut] * sign, spec_p[rows:, cut] * sign
        real, imag = product(v_re, v_im, t_re, t_im, False)
        keep(real * sign, imag * sign, col)
        real, imag = product(g_re, g_im, t_re, t_im, True)
        keep(real, imag, chans + col)
        real, imag = product(p_re, p_im, v_re, v_im, True)
        keep(real, imag, 2 * chans + col)

    def backward(index):
        cut = slice(index * chans, (index + 1) * chans)
        return (
            mm(inv_hi[...], prod_hi[:, cut])
            + mm(inv_hi[...], prod_lo[:, cut])
            + mm(inv_lo[...], prod_hi[:, cut])
        )

    def chain(own, send, got, send_sem, recv_sem, place, to):
        flying = {}

        def step(index):
            arrived = []
            for way, (length, sign) in enumerate(((3, 1), (4, -1))):
                if index > length:
                    continue
                if index:
                    flying[way, index - 1].wait_recv()
                    data = got[way, index - 1].astype(F32)
                if index == length:
                    flying[way] = data
                    continue
                mine = own[wrap(place + sign * (length - index))]
                if index:
                    mine = mine + data
                send[way, index] = mine.astype(send.dtype)
                flying[way, index] = go(
                    remote(
                        send.at[way, index],
                        got.at[way, index],
                        send_sem.at[way, index],
                        recv_sem.at[way, index],
                        "tm",
                        to(sign),
                    )
                )
            if index == 4:
                return own[place] + flying[0] + flying[1]

        return step

    for copy in later:
        copy.wait()
    lag_part[...] = (backward(2) * norm_scale).reshape(lag_part.shape)
    along_z = chain(lag_part, kz_send, kz_got, kz_send_sem, kz_recv_sem, z, at_z)
    along_y = chain(lag_row, ky_send, ky_got, ky_send_sem, ky_recv_sem, y, at_y)
    along_z(0)

    def chore(index):
        if index < 4:
            along_z(index)
        elif index == 4:
            total = along_z(4)
            lags = lag_row.shape[1]
            for at in range(RING):
                lag_row[at] = total[at * lags : (at + 1) * lags]
            along_y(0)
        elif index < 8:
            along_y(index - 4)
        else:
            kernel_grad[...] = along_y(4)

    left_v[...] = backward(1).T.astype(BF16)
    left_g[...] = (cotangent[...].astype(F32) * backward(0)).T.astype(BF16)

    parts = (part_a, part_b)
    pairs_got = (sib_a, sib_b)
    core = lax.rem(me, 2)
    chip = lax.div(me, 2)
    sibling = me + 1 - 2 * core

    def multiply(unit):
        color, slots, blocks = unit
        ref = buffers[color]
        shape = (slots[1] - slots[0], blocks[1] - blocks[0], 2, half // 2, rows)
        count = shape[0] * shape[1] * half
        cut = (slice(*slots), slice(*blocks))
        total = mm(ref[(*cut, 0)].reshape(count, chans), left_v[...])
        total = total + mm(ref[(*cut, 1)].reshape(count, chans), left_g[...])
        parts[color][cut] = total.astype(BF16).reshape(shape)
        at = (pl.ds(slots[0], shape[0]), pl.ds(blocks[0], shape[1]))
        index = UNITS.index(unit)
        return go(
            remote(
                parts[color].at[(*at, 1 - core)],
                pairs_got[color].at[at],
                sib_send.at[index],
                sib_recv.at[index],
                "chan",
                sibling,
            )
        )

    places = {slot: place for place, slot in SLOT.items()}

    def deliveries(unit):
        color, slots, blocks = unit
        group = GROUPS.index(slots)
        part = PARTS.index(blocks)
        found = []
        for slot in range(*(slots if color == 0 else blocks)):
            owner = wrap(z + places[slot])
            at = lax.rem(chip - lax.div(owner, 2) + 4, 4)
            if color == 0:
                lines = pl.ds(blocks[0], blocks[1] - blocks[0])
                src = part_a.at[slot, lines, core]
                dst = got_a.at[at, core, lines]
                sems = a_send.at[slot, part], a_recv.at[part, at, core]
            else:
                lines = pl.ds(slots[0], slots[1] - slots[0])
                src = part_b.at[lines, slot, core]
                dst = got_b.at[at, core, lines]
                sems = b_send.at[group, slot], b_recv.at[group, at, core]
            found.append((owner, src, dst, remote(src, dst, *sems, "chan", owner)))
        return found

    def finish(unit, flight):
        color, slots, blocks = unit
        flight.wait_recv()
        cut = (slice(*slots), slice(*blocks))
        total = parts[color][(*cut, core)].astype(F32) + pairs_got[color][cut].astype(F32)
        parts[color][(*cut, core)] = total.astype(BF16)
        for owner, src, dst, copy in deliveries(unit):

            @pl.when(owner != me)
            def _():
                copy.start()

            @pl.when(owner == me)
            def _():
                dst[...] = src[...]

    def needs(unit):
        color, slots, blocks = unit
        found = set()
        for slot in range(*slots):
            for block in range(*blocks):
                if slot == 0:
                    place = places[block]
                    ways = (0, 1) if place == 4 else (0,) if place < 0 else (1,)
                    if place:
                        found |= {(1, color, way, abs(place), 0) for way in ways}
                else:
                    way = (0 if block < 4 else 1) if slot == 7 else (0 if places[slot] < 0 else 1)
                    group = [low <= block < high for low, high in GROUPS].index(True)
                    found.add((2, color, way, abs(places[slot]), group))
        return found

    served = set(steps[1]) | set(steps[2])
    waiting = list(UNITS)
    pending = []

    def work():
        for unit in list(waiting):
            if needs(unit) <= served:
                waiting.remove(unit)
                pending.append((unit, multiply(unit)))
                if len(pending) > 1:
                    finish(*pending.pop(0))

    work()
    rest = [event for event in EVENTS if event not in served]
    for index, event in enumerate(rest):
        serve(event)
        served.add(event)
        work()
        if index % CHORE_EVERY == CHORE_EVERY - 1 and index // CHORE_EVERY < 8:
            chore(index // CHORE_EVERY + 1)
    assert not waiting
    for unit, flight in pending:
        finish(unit, flight)

    for at in range(4):
        for which in (0, 1) if at else (1 - core,):
            for part, (low, high) in enumerate(PARTS):
                lines = pl.ds(low, high - low)
                remote(
                    part_a.at[0, lines, 0],
                    got_a.at[at, which, lines],
                    a_send.at[0, part],
                    a_recv.at[part, at, which],
                    "chan",
                    sibling,
                ).wait_recv()
            for group, (low, high) in enumerate(GROUPS):
                lines = pl.ds(low, high - low)
                remote(
                    part_b.at[lines, 0, 0],
                    got_b.at[at, which, lines],
                    b_send.at[group, 0],
                    b_recv.at[group, at, which],
                    "chan",
                    sibling,
                ).wait_recv()

    for pair in range(RING // 2):
        pieces = []
        for place in (2 * pair, 2 * pair + 1):
            block = slot_of(wrap(place - y))
            for got in (got_a, got_b):
                for which in (0, 1):
                    total = got[0, which, block].astype(F32)
                    for at in range(1, 4):
                        total = total + got[at, which, block].astype(F32)
                    pieces.append(total)
        merged = jnp.concatenate(pieces, 0)
        out[:, 4 * half * pair : 4 * half * (pair + 1)] = merged.T.astype(BF16)

    for copy in sends:
        copy.wait_send()
    for unit in UNITS:
        for owner, src, dst, copy in deliveries(unit):

            @pl.when(owner != me)
            def _():
                copy.wait_send()


def body(norm_scale, tables, *args):
    values, _, _, taps, value_weight, _ = args
    rows, chans = values.shape
    half = value_weight.shape[0] // 2
    lags = taps.shape[0] // (RING * RING)
    assert taps.shape[0] == rows and lax.axis_size("tm") == RING * RING
    assert lax.axis_size("chan") == RING and chans == RING * 2 * half
    vmem = pl.BlockSpec(memory_space=pltpu.VMEM)
    dma = pltpu.SemaphoreType.DMA
    return pl.pallas_call(
        functools.partial(kernel, norm_scale),
        out_shape=(
            jax.ShapeDtypeStruct((rows, chans), BF16),
            jax.ShapeDtypeStruct((lags, chans), F32),
        ),
        in_specs=[pl.BlockSpec(memory_space=pl.ANY)] * 10,
        out_specs=(vmem, vmem),
        scratch_shapes=[
            pltpu.VMEM((rows, chans), BF16),
            pltpu.VMEM((rows, chans), BF16),
            pltpu.VMEM((rows, chans), BF16),
            pltpu.VMEM((rows, chans), BF16),
            *(pltpu.VMEM(table.shape, BF16) for table in tables),
            pltpu.VMEM((RING, RING, 2, half, chans), BF16),
            pltpu.VMEM((RING, RING, 2, half, chans), BF16),
            pltpu.VMEM((rows, chans), BF16),
            pltpu.VMEM((2 * rows, chans), BF16),
            pltpu.VMEM((2 * rows, chans), F32),
            pltpu.VMEM((2 * rows, chans), F32),
            pltpu.VMEM((2 * rows, chans), F32),
            pltpu.VMEM((2 * rows, chans), F32),
            pltpu.VMEM((2 * rows, 3 * chans), BF16),
            pltpu.VMEM((2 * rows, 3 * chans), BF16),
            pltpu.VMEM((chans, rows), BF16),
            pltpu.VMEM((chans, rows), BF16),
            pltpu.VMEM((RING, RING, 2, half // 2, rows), BF16),
            pltpu.VMEM((RING, RING, 2, half // 2, rows), BF16),
            pltpu.VMEM((RING, RING, half // 2, rows), BF16),
            pltpu.VMEM((RING, RING, half // 2, rows), BF16),
            pltpu.VMEM((4, 2, RING, half // 2, rows), BF16),
            pltpu.VMEM((4, 2, RING, half // 2, rows), BF16),
            pltpu.VMEM((RING, RING * lags, chans), F32),
            pltpu.VMEM((2, 4, RING * lags, chans), BF16),
            pltpu.VMEM((2, 4, RING * lags, chans), BF16),
            pltpu.VMEM((RING, lags, chans), F32),
            pltpu.VMEM((2, 4, lags, chans), F32),
            pltpu.VMEM((2, 4, lags, chans), F32),
            dma((12,)),
            dma((2,)),
            dma((2,)),
            dma((2, 2, 4)),
            dma((2, 2, 4)),
            dma((2, 2, 20)),
            dma((2, 2, 20)),
            dma((len(UNITS),)),
            dma((len(UNITS),)),
            dma((RING, len(PARTS))),
            dma((len(PARTS), 4, 2)),
            dma((len(GROUPS), RING)),
            dma((len(GROUPS), 4, 2)),
            dma((2, 4)),
            dma((2, 4)),
            dma((2, 4)),
            dma((2, 4)),
        ],
        compiler_params=pltpu.CompilerParams(
            collective_id=0, has_side_effects=True, vmem_limit_bytes=56 * 1024 * 1024
        ),
    )(*args, *tables)


def solution(mesh):
    placed = (
        P("tm", "chan"),
        P("tm", "chan"),
        P("tm", "chan"),
        P(None, "chan"),
        P("tm", "chan"),
        P("tm", "chan"),
    )

    def program(values, gates, cotangent, kernel_taps, value_weight, gate_weight):
        fwd, inv = dft_tables(kernel_taps.shape[0])
        tables = (*split_table(fwd), *split_table(inv))
        norm_scale = 1.0 / math.sqrt(values.shape[0])
        return jax.shard_map(
            lambda *args: body(norm_scale, args[6:], *args[:6]),
            mesh=mesh,
            in_specs=placed + (P(),) * 4,
            out_specs=(P("tm", "chan"), P("tm", "chan")),
            check_vma=False,
        )(values, gates, cotangent, kernel_taps, value_weight, gate_weight, *tables)

    return program
```

time: 92.7 us -> 86 us (0.928)
  Pallas kernels: 89.6 us -> 82.1 us
    pallas_call x1, Pallas kernels: 89.6 us -> 82.1 us  [body(): pl.pallas_call(functools.partial(kernel, norm_scale), out_shape=(jax.Shap...]
where the time goes in v2:
time: 86 us; the launch traced here: 85 us
  Pallas kernels  82.1 us (95%)
  local copies, waits for them, and re-layouts  2.28 us (3%)
    pallas_call x1, Pallas kernels, body(): pl.pallas_call(functools.partial(kernel, norm_scale), out_shape=(jax.Shap...  82.1 us
    unnamed x4, local copies, waits for them, and re-layouts  2.28 us

profile of v2, /device:TPU:1, one launch (start us, length us, event | category | flops | bytes accessed | tf_op | source)
XLA Modules:
  0.0 85.0 jit_solution(8874402291674004366)
XLA Ops:
  0.6 82.1 %shard_map.113 = (bf16[256,512]{1,0:T(8,128)(2,1)}, f32[4,512]{1,0:T(4,128)}) custom-call(bf16[256,512]{1,0:T(8,128)(2,1)} %values_in.1, bf16[256,512]{1,0:T(8,128)(2,1)} %gates_in.1, bf16[256,512]{1,0:T(8,128)(2,1)} %cotangent_in.1, bf16[256,512]{1,0:T(8,128)(2,1)} %taps_in.1, bf16[64,512]{1,0:T(8,128)(2,1)} %value_weight.1, bf16[64,512]{1,0:T(8,128)(2,1)} %gate_weight.1, ...), custom_call_target="tpu_custom_call" | custom-call | tf_op jit(solution)/shard_map/pallas_call | solution.py:560
  82.7 0.0 copy-start
  82.7 1.7 %copy.14 = bf16[256,512]{1,0:T(8,128)(2,1)} copy(bf16[256,512]{1,0:T(8,128)(2,1)} %get-tuple-element.4) | data formatting | bytes 524288
  84.4 0.0 copy-done
  84.4 0.6 copy.15
Async XLA Ops:
  82.7 1.7 %copy-start = (f32[4,512]{1,0:T(4,128)S(1)}, f32[4,512]{1,0:T(4,128)}, u32[]{:S(2)}) copy-start(f32[4,512]{1,0:T(4,128)} %get-tuple-element.5) | copy-start | bytes 24580

commit v3 on v2

--- a/solution.py
+++ b/solution.py
@@ -33,7 +33,7 @@
 
 
 EVENTS = arrivals()
-CHORE_EVERY = 7
+CHORES = (8, 20, 32, 44, 52, 60, 64, 68)
 
 
 def split_table(table):
@@ -496,8 +496,8 @@
         serve(event)
         served.add(event)
         work()
-        if index % CHORE_EVERY == CHORE_EVERY - 1 and index // CHORE_EVERY < 8:
-            chore(index // CHORE_EVERY + 1)
+        if index + 1 in CHORES:
+            chore(CHORES.index(index + 1) + 1)
     assert not waiting
     for unit, flight in pending:
         finish(unit, flight)

time: 86 us -> 83.5 us (0.971)
  Pallas kernels: 82.1 us -> 79 us
    pallas_call x1, Pallas kernels: 82.1 us -> 79 us  [body(): pl.pallas_call(functools.partial(kernel, norm_scale), out_shape=(jax.Shap...]
where the time goes in v3:
time: 83.5 us; the launch traced here: 81.9 us
  Pallas kernels  79 us (95%)
  local copies, waits for them, and re-layouts  2.28 us (3%)
    pallas_call x1, Pallas kernels, body(): pl.pallas_call(functools.partial(kernel, norm_scale), out_shape=(jax.Shap...  79 us
    unnamed x4, local copies, waits for them, and re-layouts  2.28 us

profile of v3, /device:TPU:1, one launch (start us, length us, event | category | flops | bytes accessed | tf_op | source)
XLA Modules:
  0.0 81.9 jit_solution(26579133310328441)
XLA Ops:
  0.6 79.0 %shard_map.113 = (bf16[256,512]{1,0:T(8,128)(2,1)}, f32[4,512]{1,0:T(4,128)}) custom-call(bf16[256,512]{1,0:T(8,128)(2,1)} %values_in.1, bf16[256,512]{1,0:T(8,128)(2,1)} %gates_in.1, bf16[256,512]{1,0:T(8,128)(2,1)} %cotangent_in.1, bf16[256,512]{1,0:T(8,128)(2,1)} %taps_in.1, bf16[64,512]{1,0:T(8,128)(2,1)} %value_weight.1, bf16[64,512]{1,0:T(8,128)(2,1)} %gate_weight.1, ...), custom_call_target="tpu_custom_call" | custom-call | tf_op jit(solution)/shard_map/pallas_call | solution.py:560
  79.6 0.0 copy-start
  79.6 1.7 %copy.14 = bf16[256,512]{1,0:T(8,128)(2,1)} copy(bf16[256,512]{1,0:T(8,128)(2,1)} %get-tuple-element.4) | data formatting | bytes 524288
  81.3 0.0 copy-done
  81.3 0.6 copy.15
Async XLA Ops:
  79.6 1.7 %copy-start = (f32[4,512]{1,0:T(4,128)S(1)}, f32[4,512]{1,0:T(4,128)}, u32[]{:S(2)}) copy-start(f32[4,512]{1,0:T(4,128)} %get-tuple-element.5) | copy-start | bytes 24580

commit v4 on v3

--- a/solution.py
+++ b/solution.py
@@ -557,7 +557,7 @@
     assert lax.axis_size("chan") == RING and chans == RING * 2 * half
     vmem = pl.BlockSpec(memory_space=pltpu.VMEM)
     dma = pltpu.SemaphoreType.DMA
-    return pl.pallas_call(
+    done = pl.pallas_call(
         functools.partial(kernel, norm_scale),
         out_shape=(
             jax.ShapeDtypeStruct((rows, chans), BF16),
@@ -618,6 +618,27 @@
         ),
     )(*args, *tables)
 
+    cuts = 4
+
+    def hand_out(total, lags_in, out, lags_out, sem):
+        copies = [pltpu.make_async_copy(lags_in, lags_out, sem.at[cuts])]
+        for index in range(cuts):
+            part = pl.ds(index * (rows // cuts), rows // cuts)
+            copies.append(pltpu.make_async_copy(total.at[part], out.at[part], sem.at[index]))
+        for copy in copies:
+            copy.start()
+        for copy in copies:
+            copy.wait()
+
+    anywhere = pl.BlockSpec(memory_space=pl.ANY)
+    return pl.pallas_call(
+        hand_out,
+        out_shape=tuple(jax.ShapeDtypeStruct(array.shape, array.dtype) for array in done),
+        in_specs=[anywhere, anywhere],
+        out_specs=(anywhere, anywhere),
+        scratch_shapes=[dma((cuts + 1,))],
+    )(*done)
+
 
 def solution(mesh):
     placed = (

time: 83.5 us -> 90.5 us (1.084)
  Pallas kernels: 79 us -> 88.3 us
  local copies, waits for them, and re-layouts: 2.28 us -> 0 us
    pallas_call x0 -> x1, Pallas kernels: none -> 9.34 us  [body(): pl.pallas_call(hand_out, out_shape=tuple((jax.ShapeDtypeStruct(array.shap...]
    unnamed x4 -> x0, local copies, waits for them, and re-layouts: 2.28 us -> none
where the time goes in v4:
time: 90.5 us; the launch traced here: 89 us
  Pallas kernels  88.3 us (98%)
    pallas_call x1, Pallas kernels, body(): pl.pallas_call(functools.partial(kernel, norm_scale), out_shape=(jax.Shap...  79 us
    pallas_call x1, Pallas kernels, body(): pl.pallas_call(hand_out, out_shape=tuple((jax.ShapeDtypeStruct(array.shap...  9.34 us

profile of v4, /device:TPU:1, one launch (start us, length us, event | category | flops | bytes accessed | tf_op | source)
XLA Modules:
  0.0 89.0 jit_solution(7602333992818250070)
XLA Ops:
  0.6 79.0 %shard_map.113 = (bf16[256,512]{1,0:T(8,128)(2,1)}, f32[4,512]{1,0:T(4,128)}) custom-call(bf16[256,512]{1,0:T(8,128)(2,1)} %values_in.1, bf16[256,512]{1,0:T(8,128)(2,1)} %gates_in.1, bf16[256,512]{1,0:T(8,128)(2,1)} %cotangent_in.1, bf16[256,512]{1,0:T(8,128)(2,1)} %taps_in.1, bf16[64,512]{1,0:T(8,128)(2,1)} %value_weight.1, bf16[64,512]{1,0:T(8,128)(2,1)} %gate_weight.1, ...), custom_call_target="tpu_custom_call" | custom-call | tf_op jit(solution)/shard_map/pallas_call | solution.py:560
  79.6 9.3 %shard_map.114 = (bf16[256,512]{1,0:T(8,128)(2,1)}, f32[4,512]{1,0:T(4,128)}) custom-call(bf16[256,512]{1,0:T(8,128)(2,1)} %get-tuple-element.4.total, f32[4,512]{1,0:T(4,128)} %get-tuple-element.5.lags_in), custom_call_target="tpu_custom_call" | custom-call | tf_op jit(solution)/shard_map/pallas_call | solution.py:634

commit v5 on v3

--- a/solution.py
+++ b/solution.py
@@ -557,7 +557,7 @@
     assert lax.axis_size("chan") == RING and chans == RING * 2 * half
     vmem = pl.BlockSpec(memory_space=pltpu.VMEM)
     dma = pltpu.SemaphoreType.DMA
-    return pl.pallas_call(
+    done = pl.pallas_call(
         functools.partial(kernel, norm_scale),
         out_shape=(
             jax.ShapeDtypeStruct((rows, chans), BF16),
@@ -618,6 +618,17 @@
         ),
     )(*args, *tables)
 
+    def hand_out(total, lags_in, out, lags_out):
+        out[...] = total[...]
+        lags_out[...] = lags_in[...]
+
+    return pl.pallas_call(
+        hand_out,
+        out_shape=tuple(jax.ShapeDtypeStruct(array.shape, array.dtype) for array in done),
+        in_specs=[vmem, vmem],
+        out_specs=(vmem, vmem),
+    )(*done)
+
 
 def solution(mesh):
     placed = (

time: 83.5 us -> 82.9 us (level)
  local copies, waits for them, and re-layouts: 2.28 us -> 0 us
  Pallas kernels: 79 us -> 80.7 us
    unnamed x4 -> x0, local copies, waits for them, and re-layouts: 2.28 us -> none
    pallas_call x0 -> x1, Pallas kernels: none -> 1.68 us  [body(): pl.pallas_call(hand_out, out_shape=tuple((jax.ShapeDtypeStruct(array.shap...]
where the time goes in v5:
time: 82.9 us; the launch traced here: 81.3 us
  Pallas kernels  80.7 us (97%)
    pallas_call x1, Pallas kernels, body(): pl.pallas_call(functools.partial(kernel, norm_scale), out_shape=(jax.Shap...  79 us
    pallas_call x1, Pallas kernels, body(): pl.pallas_call(hand_out, out_shape=tuple((jax.ShapeDtypeStruct(array.shap...  1.68 us

profile of v5, /device:TPU:1, one launch (start us, length us, event | category | flops | bytes accessed | tf_op | source)
XLA Modules:
  0.0 81.3 jit_solution(16056554238990968432)
XLA Ops:
  0.6 79.0 %shard_map.113 = (bf16[256,512]{1,0:T(8,128)(2,1)}, f32[4,512]{1,0:T(4,128)}) custom-call(bf16[256,512]{1,0:T(8,128)(2,1)} %values_in.1, bf16[256,512]{1,0:T(8,128)(2,1)} %gates_in.1, bf16[256,512]{1,0:T(8,128)(2,1)} %cotangent_in.1, bf16[256,512]{1,0:T(8,128)(2,1)} %taps_in.1, bf16[64,512]{1,0:T(8,128)(2,1)} %value_weight.1, bf16[64,512]{1,0:T(8,128)(2,1)} %gate_weight.1, ...), custom_call_target="tpu_custom_call" | custom-call | tf_op jit(solution)/shard_map/pallas_call | solution.py:560
  79.6 1.7 %shard_map.114 = (bf16[256,512]{1,0:T(8,128)(2,1)}, f32[4,512]{1,0:T(4,128)}) custom-call(bf16[256,512]{1,0:T(8,128)(2,1)} %get-tuple-element.4.total, f32[4,512]{1,0:T(4,128)} %get-tuple-element.5.lags_in), custom_call_target="tpu_custom_call" | custom-call | tf_op jit(solution)/shard_map/pallas_call | solution.py:625

commit v6 on v5

--- a/solution.py
+++ b/solution.py
@@ -278,12 +278,12 @@
     for event in EVENTS:
         steps.setdefault(event[3] + event[4], []).append(event)
 
+    for event in steps[1]:
+        serve(event)
     for copy in ahead:
         copy.wait()
     spec_t[...] = forward(True, taps[...])
     spec_p[...] = forward(True, grad_win[:rows])
-    for event in steps[1]:
-        serve(event)
     spec_v[...] = forward(False, values[...])
     for event in steps[2]:
         serve(event)

time: 82.9 us -> 82.9 us (level)
  no operation moved by 1% of the time
where the time goes in v6:
time: 82.9 us; the launch traced here: 81.3 us
  Pallas kernels  80.7 us (97%)
    pallas_call x1, Pallas kernels, body(): pl.pallas_call(functools.partial(kernel, norm_scale), out_shape=(jax.Shap...  79 us
    pallas_call x1, Pallas kernels, body(): pl.pallas_call(hand_out, out_shape=tuple((jax.ShapeDtypeStruct(array.shap...  1.68 us

profile of v6, /device:TPU:1, one launch (start us, length us, event | category | flops | bytes accessed | tf_op | source)
XLA Modules:
  0.0 81.3 jit_solution(1654486782036957671)
XLA Ops:
  0.6 79.0 %shard_map.113 = (bf16[256,512]{1,0:T(8,128)(2,1)}, f32[4,512]{1,0:T(4,128)}) custom-call(bf16[256,512]{1,0:T(8,128)(2,1)} %values_in.1, bf16[256,512]{1,0:T(8,128)(2,1)} %gates_in.1, bf16[256,512]{1,0:T(8,128)(2,1)} %cotangent_in.1, bf16[256,512]{1,0:T(8,128)(2,1)} %taps_in.1, bf16[64,512]{1,0:T(8,128)(2,1)} %value_weight.1, bf16[64,512]{1,0:T(8,128)(2,1)} %gate_weight.1, ...), custom_call_target="tpu_custom_call" | custom-call | tf_op jit(solution)/shard_map/pallas_call | solution.py:560
  79.6 1.7 %shard_map.114 = (bf16[256,512]{1,0:T(8,128)(2,1)}, f32[4,512]{1,0:T(4,128)}) custom-call(bf16[256,512]{1,0:T(8,128)(2,1)} %get-tuple-element.4.total, f32[4,512]{1,0:T(4,128)} %get-tuple-element.5.lags_in), custom_call_target="tpu_custom_call" | custom-call | tf_op jit(solution)/shard_map/pallas_call | solution.py:625
